TPU v7x, 32 devices: a whole 2x2x4 slice. The times are simulated.
32 devices in a mesh: batch: 4 (over z), token: 8 (over y, x, core).
Axes of the slice: x: 2, y: 2, z: 4, core: 2. Of those that a mesh axis runs over, the one named last changes fastest.
Arguments:
- tokens: bfloat16 [16384, 768], P(('batch', 'token')), may hold values from -9 to 9
- slot_weight: bfloat16 [768, 1024], replicated, may hold values from -2 to 2
- expert_in: bfloat16 [128, 768, 3072], P('token', None, 'batch'), may hold values from -1.7265625 to 1.7265625
- expert_out: bfloat16 [128, 3072, 768], P('token', 'batch'), may hold values from -0.6484375 to 0.6484375
Outputs:
- mixed: bfloat16 [16384, 768], P(('batch', 'token'))
All inputs are finite; a program needn't handle non-finite values.
Results may differ from a plain program's by a relative error of at most 0.023.
Values may be sent and summed in bfloat16 or wider, within the bound.
No kernel may reach another device: no remote copies, remote signals or barrier semaphores. Data moves between devices by JAX's collectives and lax.ppermute only.
A program may use at most 128 MiB of HBM per device.

v0:
```python
import jax
import jax.numpy as jnp
from jax import lax
from jax.sharding import PartitionSpec as P


def body(tokens, slot_weight, expert_in, expert_out):
    widened = tokens.astype(jnp.float32)
    scale_row = lax.rsqrt(jnp.mean(widened * widened, axis=-1, keepdims=True) + 1e-06)
    normed = (widened * scale_row).astype(jnp.bfloat16)
    logits = jnp.dot(normed, slot_weight, preferred_element_type=jnp.float32)
    column_max = lax.pmax(jnp.max(logits, axis=0), "token")
    raised = jnp.exp(logits - column_max[None, :])
    column_sum = lax.psum(jnp.sum(raised, axis=0), "token")
    dispatch = raised.astype(jnp.bfloat16)
    partial_value = jnp.einsum("ts,td->sd", dispatch, normed, preferred_element_type=jnp.float32)
    own_count = slot_weight.shape[1] // lax.axis_size("token")
    offset = lax.axis_index("token") * own_count
    own_rows = lax.psum_scatter(
        partial_value.astype(jnp.bfloat16), "token", scatter_dimension=0, tiled=True
    ).astype(jnp.float32)
    own_total = lax.dynamic_slice_in_dim(column_sum, offset, own_count, 0)
    experts_here = expert_in.shape[0]
    slot_inputs = (own_rows / own_total[:, None]).astype(jnp.bfloat16)
    slot_inputs = slot_inputs.reshape(experts_here, own_count // experts_here, tokens.shape[1])
    hidden = jnp.einsum(
        "esd,edf->esf",
        lax.all_gather(slot_inputs, "batch", axis=1, tiled=True),
        expert_in,
        preferred_element_type=jnp.float32,
    )
    hidden = jax.nn.gelu(hidden, approximate=False).astype(jnp.bfloat16)
    terms = jnp.einsum("esf,efd->esd", hidden, expert_out, preferred_element_type=jnp.float32)
    slot_outputs = lax.psum_scatter(
        terms.astype(jnp.bfloat16), "batch", scatter_dimension=1, tiled=True
    )
    combine = jax.nn.softmax(logits, axis=1).astype(jnp.bfloat16)
    slots_each = slot_outputs.shape[1]
    block_rows = lax.all_gather(slot_outputs, "token", axis=0, tiled=True)
    number = block_rows.shape[0]
    flat_rows = block_rows.reshape(number * slots_each, block_rows.shape[2])
    mixed = jnp.dot(combine, flat_rows, preferred_element_type=jnp.float32)
    return mixed.astype(jnp.bfloat16)


def solution(mesh):
    placed = (
        P(("batch", "token"), None),
        P(),
        P("token", None, "batch"),
        P("token", "batch", None),
    )
    return jax.shard_map(
        body, mesh=mesh, in_specs=placed, out_specs=P(("batch", "token"), None), check_vma=False
    )
```

profile of v0, /device:TPU:0, one launch (start us, length us, event | category | flops | bytes accessed | tf_op | source)
XLA Modules:
  0.0 166.7 jit_solution(7911845399044545035)
XLA Ops:
  6.5 0.0 copy-start
  6.5 0.0 reduce-scatter.5.cloned.1.call-start
  6.5 1.5 fusion.3
  8.0 0.1 copy-done
  8.2 0.0 copy-start.1
  8.2 3.6 %fusion.93 = (f32[512]{0:T(512)S(1)}, f32[1024]{0:T(1024)S(1)}, f32[512,1024]{1,0:T(8,128)}) fusion(bf16[768,1024]{1,0:T(8,128)(2,1)S(1)} %copy-done, bf16[512,768]{1,0:T(8,128)(2,1)} %param.4, f32[512]{0:T(512)S(1)} %add_rsqrt_fusion), kind=kOutput, calls=%fused_computation.110 | convolution fusion | flops 807533056 | bytes 4464640 | tf_op jit(solution)/shard_map/dot_general | solution.py:11
  11.8 15.1 %pmax.7 = f32[1024]{0:T(1024)S(1)} all-reduce(f32[1024]{0:T(1024)S(1)} %get-tuple-element.8), channel_id=1, replica_groups=mesh['batch'=4,'token'=8] {'token'}, use_global_device_ids=true, to_apply=%region_4.0 | all-reduce | flops 1024 | bytes 8192 | tf_op jit(solution)/shard_map/pmax | solution.py:12
  26.9 0.0 copy-done.1
  26.9 3.9 %convolution_convert_fusion = bf16[1024,768]{1,0:T(8,128)(2,1)} fusion(f32[512,1024]{1,0:T(8,128)} %get-tuple-element.11, f32[1024]{0:T(1024)S(1)} %pmax.7, bf16[512,768]{1,0:T(8,128)(2,1)S(1)} %copy-done.1, f32[512]{0:T(512)S(1)} %add_rsqrt_fusion), kind=kOutput, calls=%fused_computation.9 | convolution fusion | flops 808321024 | bytes 4462592 | tf_op jit(solution)/shard_map/ts,td->sd/dot_general | solution.py:16
  30.8 0.0 reduce-scatter.5.cloned.1.call-update
  30.8 0.0 reduce-scatter.7.cloned.1.call-start
  30.8 2.3 %fusion = (f32[512]{0:T(512)S(1)}, f32[1024]{0:T(1024)S(1)}) fusion(f32[512,1024]{1,0:T(8,128)} %get-tuple-element.11, f32[512]{0:T(512)S(1)} %get-tuple-element.7, f32[1024]{0:T(1024)S(1)} %pmax.7), kind=kLoop, calls=%fused_computation.6 | loop fusion | flops 2095616 | bytes 2109440 | tf_op jit(solution)/shard_map/reduce_sum | solution.py:37
  33.1 11.8 %psum.7 = f32[1024]{0:T(1024)S(1)} all-reduce(f32[1024]{0:T(1024)S(1)} %get-tuple-element.6), channel_id=1, replica_groups=mesh['batch'=4,'token'=8] {'token'}, use_global_device_ids=true, to_apply=%region_7.0 | all-reduce | flops 1024 | bytes 8192 | tf_op jit(solution)/shard_map/psum | solution.py:14
  44.9 0.1 dynamic_slice.3
  45.0 23.6 %reduce-scatter.5.cloned.1.call-done = bf16[128,768]{1,0:T(8,128)(2,1)} async-done(((bf16[1024,768]{1,0:T(8,128)(2,1)}), bf16[128,768]{1,0:T(8,128)(2,1)}) %reduce-scatter.5.cloned.1.call-update) | async-done | bytes 196624 | tf_op jit(solution)/shard_map/reduce_scatter | solution.py:19
  68.7 1.0 fusion.61
  69.7 19.6 %all_gather.6 = bf16[16,32,768]{2,1,0:T(8,128)(2,1)S(1)} all-gather(bf16[16,8,768]{2,1,0:T(8,128)(2,1)S(1)} %fusion.61), channel_id=1, replica_groups=mesh['batch'=4,'token'=8] {'batch'}, dimensions={1}, use_global_device_ids=true | all-gather | bytes 983040 | tf_op jit(solution)/shard_map/all_gather | solution.py:28
  89.3 8.1 %fusion.55 = (u16[32,768]{1,0:T(8,128)(2,1)S(1)}, u16[32,768]{1,0:T(8,128)(2,1)S(1)}, f32[16,32,768]{2,1,0:T(8,128)S(1)}) fusion(bf16[16,32,768]{2,1,0:T(8,128)(2,1)S(1)} %all_gather.6, bf16[16,768,768]{2,1,0:T(8,128)(2,1)} %param.6), kind=kOutput, calls=%fused_computation.71 | convolution fusion | flops 609042432 | bytes 21331968 | tf_op jit(solution)/shard_map/esd,edf->esf/dot_general | solution.py:26
  97.4 9.0 %fusion.94 = bf16[4,8,16,768]{3,1,0,2:T(8,128)(2,1)S(1)} fusion(bf16[16,768,768]{2,1,0:T(8,128)(2,1)} %param.7, f32[16,32,768]{2,1,0:T(8,128)S(1)} %get-tuple-element.12, u16[32,768]{1,0:T(8,128)(2,1)S(1)} %get-tuple-element.10, u16[32,768]{1,0:T(8,128)(2,1)S(1)} %get-tuple-element.9), kind=kOutput, calls=%fused_computation.111 | convolution fusion | flops 631898112 | bytes 21331968 | tf_op jit(solution)/shard_map/esf,efd->esd/dot_general | solution.py:33
  106.5 0.9 copy.7
  107.4 0.0 reduce-scatter.7.cloned.1.call-update
  107.4 0.0 all-gather.2.cloned.1.call-start
  107.5 21.8 %reduce-scatter.7.cloned.1.call-done = bf16[8,12288]{1,0:T(8,128)(2,1)} async-done(((bf16[32,12288]{1,0:T(8,128)(2,1)}), bf16[8,12288]{1,0:T(8,128)(2,1)}) %reduce-scatter.7.cloned.1.call-update) | async-done | bytes 196624
  129.2 1.0 copy.11
  130.2 0.7 copy.6
  130.9 0.0 all-gather.2.cloned.1.call-update
  131.0 25.3 %all-gather.2.cloned.1.call-done = bf16[128,8,768]{2,1,0:T(8,128)(2,1)} async-done(((bf16[16,8,768]{2,1,0:T(8,128)(2,1)}), bf16[128,8,768]{2,1,0:T(8,128)(2,1)}) %all-gather.2.cloned.1.call-update) | async-done | bytes 1572880 | tf_op jit(solution)/shard_map/all_gather | solution.py:39
  156.2 4.0 %fusion.16 = bf16[512,768]{1,0:T(8,128)(2,1)} fusion(bf16[128,8,768]{2,1,0:T(8,128)(2,1)} %all-gather.2.cloned.1.call-done, f32[512,1024]{1,0:T(8,128)} %get-tuple-element.11, f32[512]{0:T(512)S(1)} %get-tuple-element.5, f32[512]{0:T(512)S(1)} %get-tuple-element.7), kind=kOutput, calls=%fused_computation.35 | convolution fusion | flops 807272448 | bytes 4460544 | tf_op jit(solution)/shard_map/dot_general | solution.py:42
  (1 shorter events, 0.0 us)
Async XLA Ops:
  6.5 1.6 copy-start
  6.5 62.1 %reduce-scatter.5.cloned.1.call-start = ((), (), s32[]{:S(2)}) async-start(), calls=%async_computation.2 | async-start | bytes 1769472 | tf_op jit(solution)/shard_map/reduce_scatter | solution.py:19
  8.2 18.7 %copy-start.1 = (bf16[512,768]{1,0:T(8,128)(2,1)S(1)}, bf16[512,768]{1,0:T(8,128)(2,1)}, u32[]{:S(2)}) copy-start(bf16[512,768]{1,0:T(8,128)(2,1)} %param.4) | copy-start | bytes 2359300
  30.8 98.4 %reduce-scatter.7.cloned.1.call-start = ((), (), s32[]{:S(2)}) async-start(), calls=%async_computation.4 | async-start | bytes 983040
  107.4 48.8 %all-gather.2.cloned.1.call-start = ((), (), s32[]{:S(2)}) async-start(), calls=%async_computation.3 | async-start | bytes 1769472 | tf_op jit(solution)/shard_map/all_gather | solution.py:39
Sparse Core Ops, SparseCore 0:
  30.9 37.7 reduce-scatter.4
  107.5 21.6 reduce-scatter.6
  131.1 25.0 all-gather.1
where the time goes:
time: 167 us
  waiting for transfers between devices  70.7 us (42%)
  blocking collectives  46.5 us (28%)
  matrix products  28.6 us (17%)
  between operations  13.1 us (8%)
  other arithmetic  4.83 us (3%)
  local copies, waits for them, and re-layouts  2.86 us (2%)
    all_gather x1, waiting for transfers between devices, body(): block_rows = lax.all_gather(slot_outputs, 'token', axis=0, tiled=True)  25.3 us
    reduce_scatter x1, waiting for transfers between devices, body(): lax.psum_scatter(partial_value.astype(jnp.bfloat16), 'token', scatter_dim...  23.6 us
    unnamed x4, waiting for transfers between devices  21.8 us
    all_gather x1, blocking collectives, body(): lax.all_gather(slot_inputs, 'batch', axis=1, tiled=True)  19.6 us
    pmax x1, blocking collectives, body(): column_max = lax.pmax(jnp.max(logits, axis=0), 'token')  15.1 us
    psum x1, blocking collectives, body(): column_sum = lax.psum(jnp.sum(raised, axis=0), 'token')  11.8 us
    dot_general x1, matrix products, body(): jnp.einsum('esf,efd->esd', hidden, expert_out, preferred_element_type=jnp...  9.04 us
    dot_general x1, matrix products, body(): jnp.einsum('esd,edf->esf', lax.all_gather(slot_inputs, 'batch', axis=1, t...  8.12 us
  transfers between devices with their start and end apart: 3, of which 3 were waited for; matrix products, arithmetic and copies ran while one was open for 1% of the time, Pallas kernels for 0%

commit v1 on v0

--- a/solution.py
+++ b/solution.py
@@ -2,6 +2,28 @@
 import jax.numpy as jnp
 from jax import lax
 from jax.sharding import PartitionSpec as P
+
+
+def laid_out(blocks, dim):
+    blocks = jnp.moveaxis(blocks, 0, dim)
+    shape = blocks.shape
+    return blocks.reshape(*shape[:dim], shape[dim] * shape[dim + 1], *shape[dim + 2 :])
+
+
+def doubled(shard, axis):
+    size = lax.axis_size(axis)
+    blocks = shard[None]
+    for level in range(size.bit_length() - 1):
+        stride = 1 << level
+        theirs = lax.ppermute(blocks, axis, [(i, i ^ stride) for i in range(size)])
+        both = jnp.stack([blocks, theirs])
+        upper = lax.axis_index(axis) >> level & 1
+        blocks = jnp.where(upper == 0, both, both[::-1]).reshape(-1, *shard.shape)
+    return blocks
+
+
+def gather_by_bits(x, axis, dim):
+    return laid_out(doubled(x, axis), dim)
 
 
 def body(tokens, slot_weight, expert_in, expert_out):
@@ -36,7 +58,7 @@
     )
     combine = jax.nn.softmax(logits, axis=1).astype(jnp.bfloat16)
     slots_each = slot_outputs.shape[1]
-    block_rows = lax.all_gather(slot_outputs, "token", axis=0, tiled=True)
+    block_rows = gather_by_bits(slot_outputs, "token", 0)
     number = block_rows.shape[0]
     flat_rows = block_rows.reshape(number * slots_each, block_rows.shape[2])
     mixed = jnp.dot(combine, flat_rows, preferred_element_type=jnp.float32)

time: 167 us -> 173 us (1.036)
  starting transfers between devices: 0.09 us -> 3.19 us
  waiting for transfers between devices: 70.7 us -> 73.8 us
  matrix products: 28.6 us -> 26.5 us
    ppermute x0 -> x3, waiting for transfers between devices: none -> 28.4 us  [doubled(): theirs = lax.ppermute(blocks, axis, [(i, i ^ stride) for i in range(size)])]
    all_gather x1 -> x0, waiting for transfers between devices: 25.3 us -> none  [body(): block_rows = lax.all_gather(slot_outputs, 'token', axis=0, tiled=True)]
    ppermute x0 -> x3, starting transfers between devices: none -> 3.14 us  [doubled(): theirs = lax.ppermute(blocks, axis, [(i, i ^ stride) for i in range(size)])]
    dot_general x1, matrix products: 4 us -> 1.96 us  [body(): mixed = jnp.dot(combine, flat_rows, preferred_element_type=jnp.float32)]
    unnamed x4 -> x3, waiting for transfers between devices: 21.8 us -> 21.8 us
  transfers between devices with their start and end apart: 3 -> 5, of which waited for: 3 -> 5; matrix products, arithmetic and copies ran while one was open for 1% -> 1% of each run, Pallas kernels for 0% -> 0%
where the time goes in v1:
time: 173 us
  waiting for transfers between devices  73.8 us (43%)
  blocking collectives  46.5 us (27%)
  matrix products  26.5 us (15%)
  between operations  13.5 us (8%)
  other arithmetic  5.58 us (3%)
  local copies, waits for them, and re-layouts  3.49 us (2%)
  starting transfers between devices  3.19 us (2%)
    ppermute x3, waiting for transfers between devices, doubled(): theirs = lax.ppermute(blocks, axis, [(i, i ^ stride) for i in range(size)])  28.4 us
    reduce_scatter x1, waiting for transfers between devices, body(): lax.psum_scatter(partial_value.astype(jnp.bfloat16), 'token', scatter_dim...  23.6 us
    unnamed x3, waiting for transfers between devices  21.8 us
    all_gather x1, blocking collectives, body(): lax.all_gather(slot_inputs, 'batch', axis=1, tiled=True)  19.6 us
    pmax x1, blocking collectives, body(): column_max = lax.pmax(jnp.max(logits, axis=0), 'token')  15.1 us
    psum x1, blocking collectives, body(): column_sum = lax.psum(jnp.sum(raised, axis=0), 'token')  11.8 us
    dot_general x1, matrix products, body(): jnp.einsum('esf,efd->esd', hidden, expert_out, preferred_element_type=jnp...  9.03 us
    dot_general x1, matrix products, body(): jnp.einsum('esd,edf->esf', lax.all_gather(slot_inputs, 'batch', axis=1, t...  8.12 us
  transfers between devices with their start and end apart: 5, of which 5 were waited for; matrix products, arithmetic and copies ran while one was open for 1% of the time, Pallas kernels for 0%

profile of v1, /device:TPU:0, one launch (start us, length us, event | category | flops | bytes accessed | tf_op | source)
XLA Modules:
  0.0 172.7 jit_solution(16960355442225360237)
XLA Ops:
  6.5 1.5 fusion.3
  8.0 0.1 copy-done
  8.2 3.6 %fusion.90 = (f32[512]{0:T(512)S(1)}, f32[1024]{0:T(1024)S(1)}, f32[512,1024]{1,0:T(8,128)}) fusion(bf16[768,1024]{1,0:T(8,128)(2,1)S(1)} %copy-done, bf16[512,768]{1,0:T(8,128)(2,1)} %param.4, f32[512]{0:T(512)S(1)} %add_rsqrt_fusion), kind=kOutput, calls=%fused_computation.118 | convolution fusion | flops 807533056 | bytes 4464640 | tf_op jit(solution)/shard_map/dot_general | solution.py:33
  11.8 15.1 %pmax.7 = f32[1024]{0:T(1024)S(1)} all-reduce(f32[1024]{0:T(1024)S(1)} %get-tuple-element.8), channel_id=1, replica_groups=mesh['batch'=4,'token'=8] {'token'}, use_global_device_ids=true, to_apply=%region_4.0 | all-reduce | flops 1024 | bytes 8192 | tf_op jit(solution)/shard_map/pmax | solution.py:34
  26.9 3.9 %convolution_convert_fusion = bf16[1024,768]{1,0:T(8,128)(2,1)} fusion(f32[512,1024]{1,0:T(8,128)} %get-tuple-element.15, f32[1024]{0:T(1024)S(1)} %pmax.7, bf16[512,768]{1,0:T(8,128)(2,1)S(1)} %copy-done.2, f32[512]{0:T(512)S(1)} %add_rsqrt_fusion), kind=kOutput, calls=%fused_computation.10 | convolution fusion | flops 808321024 | bytes 4462592 | tf_op jit(solution)/shard_map/ts,td->sd/dot_general | solution.py:38
  30.8 0.0 reduce-scatter.5.cloned.1.call-update
  30.8 0.0 reduce-scatter.7.cloned.1.call-start
  30.8 2.3 %fusion = (f32[512]{0:T(512)S(1)}, f32[1024]{0:T(1024)S(1)}) fusion(f32[512,1024]{1,0:T(8,128)} %get-tuple-element.15, f32[512]{0:T(512)S(1)} %get-tuple-element.7, f32[1024]{0:T(1024)S(1)} %pmax.7), kind=kLoop, calls=%fused_computation.7 | loop fusion | flops 2095616 | bytes 2109440 | tf_op jit(solution)/shard_map/reduce_sum | solution.py:59
  33.1 11.8 %psum.7 = f32[1024]{0:T(1024)S(1)} all-reduce(f32[1024]{0:T(1024)S(1)} %get-tuple-element.6), channel_id=1, replica_groups=mesh['batch'=4,'token'=8] {'token'}, use_global_device_ids=true, to_apply=%region_7.0 | all-reduce | flops 1024 | bytes 8192 | tf_op jit(solution)/shard_map/psum | solution.py:36
  44.9 0.1 dynamic_slice.3
  45.0 23.6 %reduce-scatter.5.cloned.1.call-done = bf16[128,768]{1,0:T(8,128)(2,1)} async-done(((bf16[1024,768]{1,0:T(8,128)(2,1)}), bf16[128,768]{1,0:T(8,128)(2,1)}) %reduce-scatter.5.cloned.1.call-update) | async-done | bytes 196624 | tf_op jit(solution)/shard_map/reduce_scatter | solution.py:41
  68.7 1.0 fusion.58
  69.7 19.6 %all_gather.3 = bf16[16,32,768]{2,1,0:T(8,128)(2,1)S(1)} all-gather(bf16[16,8,768]{2,1,0:T(8,128)(2,1)S(1)} %fusion.58), channel_id=1, replica_groups=mesh['batch'=4,'token'=8] {'batch'}, dimensions={1}, use_global_device_ids=true | all-gather | bytes 983040 | tf_op jit(solution)/shard_map/all_gather | solution.py:50
  89.3 8.1 %fusion.50 = (u16[32,768]{1,0:T(8,128)(2,1)S(1)}, u16[32,768]{1,0:T(8,128)(2,1)S(1)}, f32[16,32,768]{2,1,0:T(8,128)S(1)}) fusion(bf16[16,32,768]{2,1,0:T(8,128)(2,1)S(1)} %all_gather.3, bf16[16,768,768]{2,1,0:T(8,128)(2,1)} %param.6), kind=kOutput, calls=%fused_computation.73 | convolution fusion | flops 609042432 | bytes 21331968 | tf_op jit(solution)/shard_map/esd,edf->esf/dot_general | solution.py:48
  97.4 9.0 %fusion.91 = bf16[4,8,16,768]{3,1,0,2:T(8,128)(2,1)S(1)} fusion(bf16[16,768,768]{2,1,0:T(8,128)(2,1)} %param.7, f32[16,32,768]{2,1,0:T(8,128)S(1)} %get-tuple-element.16, u16[32,768]{1,0:T(8,128)(2,1)S(1)} %get-tuple-element.10, u16[32,768]{1,0:T(8,128)(2,1)S(1)} %get-tuple-element.9), kind=kOutput, calls=%fused_computation.119 | convolution fusion | flops 631898112 | bytes 21331968 | tf_op jit(solution)/shard_map/esf,efd->esd/dot_general | solution.py:55
  106.4 0.9 copy.7
  107.4 21.8 %reduce-scatter.7.cloned.1.call-done = bf16[8,12288]{1,0:T(8,128)(2,1)} async-done(((bf16[32,12288]{1,0:T(8,128)(2,1)}), bf16[8,12288]{1,0:T(8,128)(2,1)}) %reduce-scatter.7.cloned.1.call-update) | async-done | bytes 196624
  129.2 1.0 copy.13
  130.2 0.1 copy.14
  130.2 0.1 collective-permute-start
  130.3 1.4 collective-permute-done
  131.8 0.1 fusion.57
  131.9 1.5 collective-permute-start.1
  133.4 9.7 %collective-permute-done.1 = bf16[2,16,8,768]{3,2,1,0:T(8,128)(2,1)S(1)} collective-permute-done((bf16[2,16,8,768]{3,2,1,0:T(8,128)(2,1)S(1)}, bf16[2,16,8,768]{3,2,1,0:T(8,128)(2,1)S(1)}, u32[]{:S(2)}, u32[]{:S(2)}) %collective-permute-start.1) | collective-permute-done | bytes 393248 | tf_op jit(solution)/shard_map/ppermute | solution.py:18
  143.1 0.1 pad_maximum_fusion.1
  143.2 0.1 reverse_select_fusion.1
  143.3 1.5 collective-permute-start.2
  144.9 17.2 %collective-permute-done.2 = bf16[4,16,8,768]{3,2,1,0:T(8,128)(2,1)S(1)} collective-permute-done((bf16[4,16,8,768]{3,2,1,0:T(8,128)(2,1)S(1)}, bf16[4,16,8,768]{3,2,1,0:T(8,128)(2,1)S(1)}, u32[]{:S(2)}, u32[]{:S(2)}) %collective-permute-start.2) | collective-permute-done | bytes 786464 | tf_op jit(solution)/shard_map/ppermute | solution.py:18
  162.1 0.1 pad_maximum_fusion
  162.3 0.3 reverse_select_fusion
  162.5 1.3 copy-done.1
  163.9 2.0 %convolution_convert_fusion.1 = bf16[512,768]{1,0:T(8,128)(2,1)} fusion(bf16[1024,768]{1,0:T(8,128)(2,1)S(1)} %bitcast.37, f32[512,1024]{1,0:T(8,128)S(1)} %copy-done.1, f32[512]{0:T(512)S(1)} %get-tuple-element.5, f32[512]{0:T(512)S(1)} %get-tuple-element.7), kind=kOutput, calls=%fused_computation.35 | convolution fusion | flops 807272448 | bytes 4460544 | tf_op jit(solution)/shard_map/dot_general | solution.py:64
  (8 shorter events, 0.1 us)
Async XLA Ops:
  6.5 1.6 copy-start
  6.5 62.1 %reduce-scatter.5.cloned.1.call-start = ((), (), s32[]{:S(2)}) async-start(), calls=%async_computation.2 | async-start | bytes 1769472 | tf_op jit(solution)/shard_map/reduce_scatter | solution.py:41
  8.2 18.7 %copy-start.2 = (bf16[512,768]{1,0:T(8,128)(2,1)S(1)}, bf16[512,768]{1,0:T(8,128)(2,1)}, u32[]{:S(2)}) copy-start(bf16[512,768]{1,0:T(8,128)(2,1)} %param.4) | copy-start | bytes 2359300
  30.8 98.4 %reduce-scatter.7.cloned.1.call-start = ((), (), s32[]{:S(2)}) async-start(), calls=%async_computation.3 | async-start | bytes 983040
  130.2 1.5 collective-permute-start
  131.9 11.2 %collective-permute-start.1 = (bf16[2,16,8,768]{3,2,1,0:T(8,128)(2,1)S(1)}, bf16[2,16,8,768]{3,2,1,0:T(8,128)(2,1)S(1)}, u32[]{:S(2)}, u32[]{:S(2)}) collective-permute-start(bf16[2,16,8,768]{3,2,1,0:T(8,128)(2,1)S(1)} %get-tuple-element.12), channel_id=1, source_target_pairs={{0,2},{1,3},{2,0},{3,1},{4,6},{5,7},{6,4},{7,5},{8,10},{9,11},{10,... | collective-permute-start | bytes 1179656 | tf_op jit(solution)/shard_map/ppermute | solution.py:18
  143.3 18.8 %collective-permute-start.2 = (bf16[4,16,8,768]{3,2,1,0:T(8,128)(2,1)S(1)}, bf16[4,16,8,768]{3,2,1,0:T(8,128)(2,1)S(1)}, u32[]{:S(2)}, u32[]{:S(2)}) collective-permute-start(bf16[4,16,8,768]{3,2,1,0:T(8,128)(2,1)S(1)} %bitcast.35), channel_id=1, source_target_pairs={{0,4},{1,5},{2,6},{3,7},{4,0},{5,1},{6,2},{7,3},{8,12},{9,13},{10,... | collective-permute-start | bytes 2359304 | tf_op jit(solution)/shard_map/ppermute | solution.py:18
  162.3 1.6 copy-start.1
Sparse Core Ops, SparseCore 0:
  30.9 37.7 reduce-scatter.4
  107.5 21.6 reduce-scatter.6
